TPU v7x, 256 devices: a whole 4x4x8 slice. The times are simulated.
256 devices in a mesh: fsdp: 32 (over z_lo, x, core), seq: 8 (over y, z_hi).
Axes of the slice: x: 4, y: 4, z: 8 (z_hi: 2, z_lo: 4; z = z_hi * 4 + z_lo), core: 2. Of those that a mesh axis runs over, the one named last changes fastest.
Arguments:
- queries: bfloat16 [32768, 3072], P(('fsdp', 'seq')), may hold values from -1000 to 1000
- keys: bfloat16 [32768, 3072], P(('fsdp', 'seq')), may hold values from -1000 to 1000
- values: bfloat16 [32768, 3072], P(('fsdp', 'seq')), may hold values from -6 to 6
- image_ids: int32 [32, 1024], P('fsdp'), may hold values from 0 to 15, never falling along the last dimension, each value on 1 to 512 neighbouring positions
- q_gain: float32 [128], replicated, may hold values from 0.6 to 6
- k_gain: float32 [128], replicated, may hold values from 0.6 to 6
- w_out: bfloat16 [3072, 6144], P('fsdp', 'seq'), may hold values from -0.109375 to 0.109375
- grad_y: bfloat16 [32768, 6144], P('fsdp', 'seq'), may hold values from -6 to 6
Outputs:
- grad_queries: bfloat16 [32768, 24, 128], P('fsdp', 'seq')
- grad_keys: bfloat16 [32768, 24, 128], P('fsdp', 'seq')
- grad_values: bfloat16 [32768, 24, 128], P('fsdp', 'seq')
- grad_w: float32 [3072, 6144], P('fsdp', 'seq')
All inputs are finite; a program needn't handle non-finite values.
Results may differ from a plain program's by a relative error of at most 0.02.
The roundings to bfloat16 on the way count: a program that leaves them out, or rounds other values in their place, can miss the bound.
Values may be sent and summed in bfloat16 or wider, within the bound.
A program may use at most 128 MiB of HBM per device.

v0:
```python
import jax
import jax.numpy as jnp
from jax import lax
from jax.sharding import PartitionSpec as P


def norm_parts(source, gain):
    wide = source.astype(jnp.float32)
    centred = wide - jnp.mean(wide, axis=-1, keepdims=True)
    scale_inv = lax.rsqrt(jnp.mean(centred * centred, axis=-1, keepdims=True) + 1e-06)
    x_hat = centred * scale_inv
    return (x_hat, scale_inv, (x_hat * gain).astype(jnp.bfloat16))


def norm_back(grad_n, x_hat, scale_inv, gain):
    scaled = grad_n * gain
    return scale_inv * (
        scaled
        - jnp.mean(scaled, axis=-1, keepdims=True)
        - x_hat * jnp.mean(scaled * x_hat, axis=-1, keepdims=True)
    )


def probabilities(normalized_queries, normalized_keys, same_image, scale_factor):
    scores = (
        jnp.einsum(
            "krt,irt->rki", normalized_queries, normalized_keys, preferred_element_type=jnp.float32
        )
        * scale_factor
    )
    scores = jnp.where(same_image[None], scores, -1e30)
    row_top = jnp.max(scores, axis=-1, keepdims=True)
    exp_terms = jnp.exp(scores - row_top)
    return exp_terms / jnp.sum(exp_terms, axis=-1, keepdims=True)


def local(queries, keys, values, image_ids, q_gain, k_gain, w_out, grad_y):
    head_dim = q_gain.shape[0]
    tok_rows = queries.shape[0]
    heads_all = queries.shape[1] // head_dim
    scale_factor = head_dim ** (-0.5)
    q_patch = queries.reshape(tok_rows, heads_all, head_dim)
    k_patch = keys.reshape(tok_rows, heads_all, head_dim)
    v_patch = values.reshape(tok_rows, heads_all, head_dim)
    q_local, k_local, value_shard = (
        lax.all_to_all(q_patch, "seq", split_axis=1, concat_axis=0, tiled=True),
        lax.all_to_all(k_patch, "seq", split_axis=1, concat_axis=0, tiled=True),
        lax.all_to_all(v_patch, "seq", split_axis=1, concat_axis=0, tiled=True),
    )
    seq_length = q_local.shape[0]
    local_heads = q_local.shape[1]
    image_row = image_ids[0]
    same_image = image_row[:, None] == image_row[None, :]
    q_hat, q_inv, normalized_queries = norm_parts(q_local, q_gain)
    k_hat, k_inv, normalized_keys = norm_parts(k_local, k_gain)
    prob_rows = probabilities(normalized_queries, normalized_keys, same_image, scale_factor)
    probs_reduced_precision = prob_rows.astype(jnp.bfloat16)
    attended = jnp.einsum(
        "tgi,itp->gtp", probs_reduced_precision, value_shard, preferred_element_type=jnp.float32
    ).astype(jnp.bfloat16)
    attended_flat = attended.reshape(seq_length, local_heads * head_dim)
    partial_g = jnp.einsum(
        "ld,cd->lc",
        grad_y,
        lax.all_gather(w_out, "fsdp", axis=0, tiled=True),
        preferred_element_type=jnp.float32,
    )
    grad_sum = lax.psum_scatter(
        partial_g.astype(jnp.bfloat16), "seq", scatter_dimension=1, tiled=True
    )
    attention_gradient = grad_sum.reshape(seq_length, local_heads, head_dim)
    grad_values = jnp.einsum(
        "jpw,pjy->wjy",
        probs_reduced_precision,
        attention_gradient,
        preferred_element_type=jnp.float32,
    ).astype(jnp.bfloat16)
    probability_gradient = jnp.einsum(
        "krt,irt->rki", attention_gradient, value_shard, preferred_element_type=jnp.float32
    )
    row_delta = jnp.sum(prob_rows * probability_gradient, axis=-1, keepdims=True)
    score_gradient = (prob_rows * (probability_gradient - row_delta) * scale_factor).astype(
        jnp.bfloat16
    )
    normed_query_gradient = jnp.einsum(
        "tgi,itp->gtp", score_gradient, normalized_keys, preferred_element_type=jnp.float32
    )
    normed_key_gradient = jnp.einsum(
        "jpw,pjy->wjy", score_gradient, normalized_queries, preferred_element_type=jnp.float32
    )
    grad_queries = norm_back(normed_query_gradient, q_hat, q_inv, q_gain).astype(jnp.bfloat16)
    grad_keys = norm_back(normed_key_gradient, k_hat, k_inv, k_gain).astype(jnp.bfloat16)
    partial_w = jnp.einsum(
        "lc,ld->cd",
        lax.all_gather(attended_flat, "seq", axis=1, tiled=True),
        grad_y,
        preferred_element_type=jnp.float32,
    )
    summed = lax.psum_scatter(partial_w, "fsdp", scatter_dimension=0, tiled=True)
    grad_w = summed * seq_length ** (-0.5)
    return (grad_queries, grad_keys, grad_values, grad_w)


def solution(mesh):
    in_specs = (
        P(("fsdp", "seq"), None),
        P(("fsdp", "seq"), None),
        P(("fsdp", "seq"), None),
        P("fsdp", None),
        P(),
        P(),
        P("fsdp", "seq"),
        P("fsdp", "seq"),
    )
    out_specs = (
        P("fsdp", "seq", None),
        P("fsdp", "seq", None),
        P("fsdp", "seq", None),
        P("fsdp", "seq"),
    )
    return jax.shard_map(local, mesh=mesh, in_specs=in_specs, out_specs=out_specs, check_vma=False)
```

profile of v0, /device:TPU:8, one launch (start us, length us, event | category | flops | bytes accessed | tf_op | source)
XLA Modules:
  0.0 586.4 jit_solution(3500788171164991081)
XLA Ops:
  7.9 2.4 copy.60
  10.3 11.5 %all-to-all-start = ((bf16[128,24,128]{0,2,1:T(8,128)(2,1)}), bf16[128,24,128]{0,2,1:T(8,128)(2,1)S(1)}, u32[]{:S(2)}, u32[]{:S(2)}) async-start(bf16[128,24,128]{0,2,1:T(8,128)(2,1)} %bitcast), calls=%async_computation | async-start | bytes 1572864 | tf_op jit(solution)/shard_map/all_to_all | solution.py:46
  23.0 23.3 %all-to-all-done = bf16[128,24,128]{0,2,1:T(8,128)(2,1)S(1)} async-done(((bf16[128,24,128]{0,2,1:T(8,128)(2,1)}), bf16[128,24,128]{0,2,1:T(8,128)(2,1)S(1)}, u32[]{:S(2)}, u32[]{:S(2)}) %all-to-all-start) | async-done | bytes 786464 | tf_op jit(solution)/shard_map/all_to_all | solution.py:46
  46.3 6.4 %all-to-all-start.1 = ((bf16[128,24,128]{0,2,1:T(8,128)(2,1)}), bf16[128,24,128]{0,2,1:T(8,128)(2,1)S(1)}, u32[]{:S(2)}, u32[]{:S(2)}) async-start(bf16[128,24,128]{0,2,1:T(8,128)(2,1)} %bitcast.107), calls=%async_computation.1 | async-start | bytes 1572864 | tf_op jit(solution)/shard_map/all_to_all | solution.py:47
  52.7 2.3 copy.69
  55.0 11.3 %all-to-all-done.1 = bf16[128,24,128]{0,2,1:T(8,128)(2,1)S(1)} async-done(((bf16[128,24,128]{0,2,1:T(8,128)(2,1)}), bf16[128,24,128]{0,2,1:T(8,128)(2,1)S(1)}, u32[]{:S(2)}, u32[]{:S(2)}) %all-to-all-start.1) | async-done | bytes 786464 | tf_op jit(solution)/shard_map/all_to_all | solution.py:47
  66.3 7.3 %all-to-all-start.2 = ((bf16[128,24,128]{0,2,1:T(8,128)(2,1)}), bf16[128,24,128]{0,2,1:T(8,128)(2,1)}, u32[]{:S(2)}, u32[]{:S(2)}) async-start(bf16[128,24,128]{0,2,1:T(8,128)(2,1)} %bitcast.106), calls=%async_computation.2 | async-start | bytes 1572864 | tf_op jit(solution)/shard_map/all_to_all | solution.py:48
  73.7 1.7 broadcast_compare_fusion
  75.4 1.4 copy.61
  78.5 1.4 copy.63
  80.4 9.0 %all-to-all-done.2 = bf16[128,24,128]{0,2,1:T(8,128)(2,1)} async-done(((bf16[128,24,128]{0,2,1:T(8,128)(2,1)}), bf16[128,24,128]{0,2,1:T(8,128)(2,1)}, u32[]{:S(2)}, u32[]{:S(2)}) %all-to-all-start.2) | async-done | bytes 786464 | tf_op jit(solution)/shard_map/all_to_all | solution.py:48
  89.4 2.3 copy.71
  91.7 1.4 convert_element_type.96
  93.3 2.3 copy-done.3
  97.6 1.6 multiply_convert_fusion.1
  99.2 11.0 %fusion.54 = (f32[3,1024]{1,0:T(4,128)S(1)}, f32[3,1024,1024]{1,2,0:T(8,128)}) fusion(pred[1024,1024]{0,1:T(8,128)(4,1)S(1)} %copy-done.12, bf16[1024,3,128]{0,2,1:T(8,128)(2,1)} %get-tuple-element.32, bf16[1024,3,128]{0,2,1:T(8,128)(2,1)} %get-tuple-element.33), kind=kOutput, calls=%fused_computation.65 | convolution fusion | flops 817890304 | bytes 15216640 | tf_op jit(solution)/shard_map/sub | solution.py:33
  110.2 6.6 %fusion.38 = bf16[3,1024,128]{1,2,0:T(8,128)(2,1)} fusion(bf16[1024,3,128]{2,0,1:T(8,128)(2,1)S(1)} %bitcast.104, f32[3,1024,1024]{1,2,0:T(8,128)} %get-tuple-element.29, f32[3,1024]{1,0:T(4,128)S(1)} %get-tuple-element.28), kind=kOutput, calls=%fused_computation.45 | convolution fusion | flops 811991040 | bytes 14168064 | tf_op jit(solution)/shard_map/tgi,itp->gtp/dot_general | solution.py:58
  117.1 9.4 %convolution_convert_fusion = bf16[1024,3072]{1,0:T(8,128)(2,1)} fusion(bf16[1024,768]{1,0:T(8,128)(2,1)S(1)} %copy-done, bf16[3072,768]{1,0:T(8,128)(2,1)} %all-gather.3.cloned.1.call-done), kind=kOutput, calls=%fused_computation.14 | convolution fusion | flops 4834983936 | bytes 12582912 | tf_op jit(solution)/shard_map/ld,cd->lc/dot_general | solution.py:62
  126.5 8.7 %copy.92 = bf16[1024,3072]{0,1:T(8,128)(2,1)} copy(bf16[1024,3072]{1,0:T(8,128)(2,1)} %convolution_convert_fusion) | data formatting | bytes 12582912
  135.2 130.9 %all-gather.5.cloned.1.call-done = bf16[1024,3072]{0,1:T(8,128)(2,1)} async-done(((bf16[1024,384]{0,1:T(8,128)(2,1)}), bf16[1024,3072]{0,1:T(8,128)(2,1)}) %all-gather.5.cloned.1.call-update) | async-done | bytes 6291472 | tf_op jit(solution)/shard_map/all_gather | solution.py:95
  266.1 10.0 %fusion.59 = f32[3072,768]{1,0:T(8,128)} fusion(bf16[1024,3072]{0,1:T(8,128)(2,1)} %all-gather.5.cloned.1.call-done, bf16[1024,768]{1,0:T(8,128)(2,1)S(1)} %copy-done), kind=kOutput, calls=%fused_computation.66 | convolution fusion | flops 4831838208 | bytes 17301504 | tf_op jit(solution)/shard_map/lc,ld->cd/dot_general | solution.py:93
  276.1 143.7 %reduce-scatter.7.cloned.1.call-done = bf16[384,1024]{1,0:T(8,128)(2,1)} async-done(((bf16[3072,1024]{1,0:T(8,128)(2,1)}), bf16[384,1024]{1,0:T(8,128)(2,1)}) %reduce-scatter.7.cloned.1.call-update) | async-done | bytes 786448
  419.8 7.5 %fusion.60 = f32[3,1024,1024]{1,2,0:T(8,128)} fusion(bf16[1024,3,128]{2,0,1:T(8,128)(2,1)S(1)} %bitcast.105, bf16[1024,3,128]{0,2,1:T(8,128)(2,1)} %bitcast.108), kind=kOutput, calls=%fused_computation.67 | convolution fusion | flops 805306368 | bytes 14155776 | tf_op jit(solution)/shard_map/krt,irt->rki/dot_general | solution.py:78
  427.3 19.4 %bitcast_reduce_fusion.1 = (f32[1024,3]{0,1:T(4,128)S(1)}, f32[1024,3]{0,1:T(4,128)S(1)}, f32[3,128,1024]{2,1,0:T(8,128)}) fusion(f32[1024,3]{0,1:T(4,128)S(1)} %rsqrt_bitcast_fusion.1, f32[1024,3]{0,1:T(4,128)S(1)} %get-tuple-element.25, f32[8,3,16,8,128]{4,3,2,1,0:T(8,128)S(1)} %bitcast.102, f32[128]{0:T(128)S(1)} %copy-done.18, ...), kind=kOutput, calls=%fused_computation.33 | convolution fusion | flops 829683712 | bytes 29159936 | tf_op jit(solution)/shard_map/tgi,itp->gtp/dot_general | solution.py:85
  446.7 1.8 fusion.27
  448.6 1.2 copy.78
  450.3 19.6 %bitcast_reduce_fusion = (f32[1024,3]{0,1:T(4,128)S(1)}, f32[1024,3]{0,1:T(4,128)S(1)}, f32[3,128,1024]{2,1,0:T(8,128)}) fusion(f32[1024,3]{0,1:T(4,128)S(1)} %rsqrt_bitcast_fusion, f32[1024,3]{0,1:T(4,128)S(1)} %get-tuple-element.26, f32[8,3,16,8,128]{4,3,2,1,0:T(8,128)S(1)} %bitcast.99, f32[128]{0:T(128)S(1)} %copy-done.19, ...), kind=kOutput, calls=%fused_computation.26 | convolution fusion | flops 829683712 | bytes 29159936 | tf_op jit(solution)/shard_map/jpw,pjy->wjy/dot_general | solution.py:88
  469.9 1.7 fusion.23
  471.7 1.2 copy.79
  472.8 7.0 %fusion.43 = bf16[1024,3,128]{0,2,1:T(8,128)(2,1)S(1)} fusion(bf16[1024,3,128]{0,2,1:T(8,128)(2,1)S(1)} %bitcast.109, f32[3,1024,1024]{1,2,0:T(8,128)} %get-tuple-element.29, f32[3,1024]{1,0:T(4,128)S(1)} %get-tuple-element.28), kind=kOutput, calls=%fused_computation.47 | convolution fusion | flops 811991040 | bytes 14168064 | tf_op jit(solution)/shard_map/jpw,pjy->wjy/dot_general | solution.py:72
  481.1 97.2 %reduce-scatter.5.cloned.1.call-done = f32[96,768]{1,0:T(8,128)} async-done(((f32[3072,768]{1,0:T(8,128)}), f32[96,768]{1,0:T(8,128)}) %reduce-scatter.5.cloned.1.call-update) | async-done | bytes 294928 | tf_op jit(solution)/shard_map/reduce_scatter | solution.py:99
  578.2 1.7 broadcast_multiply_fusion
  (63 shorter events, 8.2 us)
Async XLA Ops:
  7.2 109.9 %copy-start = (bf16[1024,768]{1,0:T(8,128)(2,1)S(1)}, bf16[1024,768]{1,0:T(8,128)(2,1)}, u32[]{:S(2)}) copy-start(bf16[1024,768]{1,0:T(8,128)(2,1)} %param.15) | copy-start | bytes 4718596
  7.2 109.9 %all-gather.3.cloned.1.call-start = ((), (), s32[]{:S(2)}) async-start(), calls=%async_computation.5 | async-start | bytes 4866048 | tf_op jit(solution)/shard_map/all_gather | solution.py:65
  7.9 13.9 %copy-start.14 = (bf16[128,3072]{1,0:T(8,128)(2,1)S(1)}, bf16[128,3072]{1,0:T(8,128)(2,1)}, u32[]{:S(2)}) copy-start(bf16[128,3072]{1,0:T(8,128)(2,1)} %param.9) | copy-start | bytes 2359300
  10.3 36.0 %all-to-all-start = ((bf16[128,24,128]{0,2,1:T(8,128)(2,1)}), bf16[128,24,128]{0,2,1:T(8,128)(2,1)S(1)}, u32[]{:S(2)}, u32[]{:S(2)}) async-start(bf16[128,24,128]{0,2,1:T(8,128)(2,1)} %bitcast), calls=%async_computation | async-start | bytes 1572864 | tf_op jit(solution)/shard_map/all_to_all | solution.py:46
  46.3 8.7 %copy-start.8 = (bf16[128,24,128]{0,2,1:T(8,128)(2,1)}, bf16[128,24,128]{0,2,1:T(8,128)(2,1)S(1)}, u32[]{:S(2)}) copy-start(bf16[128,24,128]{0,2,1:T(8,128)(2,1)S(1)} %all-to-all-done) | copy-start | bytes 2359300
  46.3 20.0 %all-to-all-start.1 = ((bf16[128,24,128]{0,2,1:T(8,128)(2,1)}), bf16[128,24,128]{0,2,1:T(8,128)(2,1)S(1)}, u32[]{:S(2)}, u32[]{:S(2)}) async-start(bf16[128,24,128]{0,2,1:T(8,128)(2,1)} %bitcast.107), calls=%async_computation.1 | async-start | bytes 1572864 | tf_op jit(solution)/shard_map/all_to_all | solution.py:47
  52.7 21.0 %copy-start.17 = (s32[1,1024]{1,0:T(1,128)S(1)}, s32[1,1024]{1,0:T(1,128)}, u32[]{:S(2)}) copy-start(s32[1,1024]{1,0:T(1,128)} %param.11) | copy-start | bytes 12292
  66.3 7.3 %copy-start.9 = (bf16[128,24,128]{0,2,1:T(8,128)(2,1)}, bf16[128,24,128]{0,2,1:T(8,128)(2,1)S(1)}, u32[]{:S(2)}) copy-start(bf16[128,24,128]{0,2,1:T(8,128)(2,1)S(1)} %all-to-all-done.1) | copy-start | bytes 2359300
  66.3 23.1 %all-to-all-start.2 = ((bf16[128,24,128]{0,2,1:T(8,128)(2,1)}), bf16[128,24,128]{0,2,1:T(8,128)(2,1)}, u32[]{:S(2)}, u32[]{:S(2)}) async-start(bf16[128,24,128]{0,2,1:T(8,128)(2,1)} %bitcast.106), calls=%async_computation.2 | async-start | bytes 1572864 | tf_op jit(solution)/shard_map/all_to_all | solution.py:48
  73.7 192.5 %all-gather.5.cloned.1.call-start = ((), (), s32[]{:S(2)}) async-start(), calls=%async_computation.6 | async-start | bytes 7077888 | tf_op jit(solution)/shard_map/all_gather | solution.py:95
  76.8 1.1 copy-start.2
  91.7 1.4 copy-start.10
  93.1 4.5 copy-start.6
  93.1 2.5 copy-start.3
  93.3 4.3 copy-start.4
  95.6 1.9 copy-start.18
  95.6 1.9 copy-start.19
  97.6 1.6 copy-start.12
  99.2 11.0 %copy-start.11 = (bf16[8,128,3,128]{3,1,0,2:T(8,128)(2,1)S(1)}, bf16[8,128,3,128]{3,1,0,2:T(8,128)(2,1)}, u32[]{:S(2)}) copy-start(bf16[8,128,3,128]{3,1,0,2:T(8,128)(2,1)} %copy.71) | copy-start | bytes 2359300
  116.8 302.9 %reduce-scatter.7.cloned.1.call-start = ((), (), s32[]{:S(2)}) async-start(), calls=%async_computation.8 | async-start | bytes 7077888
  135.2 443.0 %reduce-scatter.5.cloned.1.call-start = ((), (), s32[]{:S(2)}) async-start(), calls=%async_computation.7 | async-start | bytes 9732096 | tf_op jit(solution)/shard_map/reduce_scatter | solution.py:99
  419.8 7.6 %copy-start.7 = (f32[128,24,128]{0,2,1:T(8,128)S(1)}, f32[128,24,128]{0,2,1:T(8,128)}, u32[]{:S(2)}) copy-start(f32[128,24,128]{0,2,1:T(8,128)} %copy-done.6) | copy-start | bytes 4718596
  419.8 7.6 %copy-start.16 = (bf16[1024,3,128]{0,2,1:T(8,128)(2,1)S(1)}, bf16[1024,3,128]{0,2,1:T(8,128)(2,1)}, u32[]{:S(2)}) copy-start(bf16[1024,3,128]{0,2,1:T(8,128)(2,1)} %get-tuple-element.33) | copy-start | bytes 2359300
  446.7 3.0 copy-start.15
  448.6 1.7 copy-start.5
  471.7 1.2 copy-start.13
  472.8 107.1 %copy-start.1 = (bf16[1024,768]{1,0:T(8,128)(2,1)S(1)}, bf16[1024,768]{1,0:T(8,128)(2,1)}, u32[]{:S(2)}) copy-start(bf16[1024,768]{1,0:T(8,128)(2,1)} %param.15) | copy-start | bytes 4718596
Sparse Core Ops, SparseCore 0:
  9.9 106.4 all-gather.2
  119.6 146.5 all-gather.4
  270.3 149.3 reduce-scatter.6
  422.4 155.7 reduce-scatter.4
where the time goes:
time: 587 us; the launch traced here: 586 us
  waiting for transfers between devices  416 us (71%)
  matrix products  90.5 us (15%)
  local copies, waits for them, and re-layouts  27.2 us (5%)
  starting transfers between devices  25.6 us (4%)
  between operations  14 us (2%)
  other arithmetic  13 us (2%)
    unnamed x5, waiting for transfers between devices  144 us
    all_gather x1, waiting for transfers between devices, local(): lax.all_gather(attended_flat, 'seq', axis=1, tiled=True)  131 us
    reduce_scatter x1, waiting for transfers between devices, local(): lax.psum_scatter(partial_w, 'fsdp', scatter_dimension=0, tiled=True)  97.2 us
    all_to_all x1, waiting for transfers between devices, local(): lax.all_to_all(q_patch, 'seq', split_axis=1, concat_axis=0, tiled=True)  23.3 us
    unnamed x47, local copies, waits for them, and re-layouts  22.1 us
    dot_general x1, matrix products, local(): jnp.einsum('jpw,pjy->wjy', score_gradient, normalized_queries, preferred_...  19.6 us
    dot_general x1, matrix products, local(): jnp.einsum('tgi,itp->gtp', score_gradient, normalized_keys, preferred_ele...  19.4 us
  transfers between devices with their start and end apart: 7, of which 6 were waited for; matrix products, arithmetic and copies ran while one was open for 21% of the time, Pallas kernels for 0%

commit v1 on v0

--- a/solution.py
+++ b/solution.py
@@ -92,7 +92,9 @@
     grad_keys = norm_back(normed_key_gradient, k_hat, k_inv, k_gain).astype(jnp.bfloat16)
     partial_w = jnp.einsum(
         "lc,ld->cd",
-        lax.all_gather(attended_flat, "seq", axis=1, tiled=True),
+        jnp.concatenate(
+            lax.all_to_all(jnp.stack([attended_flat] * lax.axis_size("seq")), "seq", 0, 0), axis=1
+        ),
         grad_y,
         preferred_element_type=jnp.float32,
     )

time: 587 us -> 556 us (0.947)
  waiting for transfers between devices: 416 us -> 168 us
  blocking collectives: 0 us -> 219 us
    all_to_all x0 -> x1, blocking collectives: none -> 219 us  [local(): lax.all_to_all(jnp.stack([attended_flat] * lax.axis_size('seq')), 'seq',...]
    all_gather x1 -> x0, waiting for transfers between devices: 131 us -> none  [local(): lax.all_gather(attended_flat, 'seq', axis=1, tiled=True)]
    unnamed x5 -> x4, waiting for transfers between devices: 144 us -> 20.5 us
    all_gather x1, waiting for transfers between devices: 0.02 us -> 6.71 us  [local(): lax.all_gather(w_out, 'fsdp', axis=0, tiled=True)]
    unnamed x47 -> x43, local copies, waits for them, and re-layouts: 22.1 us -> 23 us
  transfers between devices with their start and end apart: 7 -> 6, of which waited for: 6 -> 6; matrix products, arithmetic and copies ran while one was open for 21% -> 19% of each run, Pallas kernels for 0% -> 0%
where the time goes in v1:
time: 556 us; the launch traced here: 554 us
  blocking collectives  219 us (39%)
  waiting for transfers between devices  168 us (30%)
  matrix products  86.8 us (16%)
  local copies, waits for them, and re-layouts  28.9 us (5%)
  starting transfers between devices  25.5 us (5%)
  between operations  14 us (3%)
  other arithmetic  12.6 us (2%)
    all_to_all x1, blocking collectives, local(): lax.all_to_all(jnp.stack([attended_flat] * lax.axis_size('seq')), 'seq',...  219 us
    reduce_scatter x1, waiting for transfers between devices, local(): lax.psum_scatter(partial_w, 'fsdp', scatter_dimension=0, tiled=True)  96.8 us
    all_to_all x1, waiting for transfers between devices, local(): lax.all_to_all(q_patch, 'seq', split_axis=1, concat_axis=0, tiled=True)  23.3 us
    unnamed x43, local copies, waits for them, and re-layouts  23 us
    unnamed x4, waiting for transfers between devices  20.5 us
    dot_general x1, matrix products, local(): jnp.einsum('tgi,itp->gtp', score_gradient, normalized_keys, preferred_ele...  19.6 us
    dot_general x1, matrix products, local(): jnp.einsum('jpw,pjy->wjy', score_gradient, normalized_queries, preferred_...  19.6 us
    all_to_all x1, starting transfers between devices, local(): lax.all_to_all(q_patch, 'seq', split_axis=1, concat_axis=0, tiled=True)  11.5 us
  transfers between devices with their start and end apart: 6, of which 6 were waited for; matrix products, arithmetic and copies ran while one was open for 19% of the time, Pallas kernels for 0%

profile of v1, /device:TPU:8, one launch (start us, length us, event | category | flops | bytes accessed | tf_op | source)
XLA Modules:
  0.0 554.5 jit_solution(1334746391870315241)
XLA Ops:
  7.9 2.4 copy.61
  10.3 11.5 %all-to-all-start = ((bf16[128,24,128]{0,2,1:T(8,128)(2,1)}), bf16[128,24,128]{0,2,1:T(8,128)(2,1)S(1)}, u32[]{:S(2)}, u32[]{:S(2)}) async-start(bf16[128,24,128]{0,2,1:T(8,128)(2,1)} %bitcast), calls=%async_computation | async-start | bytes 1572864 | tf_op jit(solution)/shard_map/all_to_all | solution.py:46
  23.0 23.3 %all-to-all-done = bf16[128,24,128]{0,2,1:T(8,128)(2,1)S(1)} async-done(((bf16[128,24,128]{0,2,1:T(8,128)(2,1)}), bf16[128,24,128]{0,2,1:T(8,128)(2,1)S(1)}, u32[]{:S(2)}, u32[]{:S(2)}) %all-to-all-start) | async-done | bytes 786464 | tf_op jit(solution)/shard_map/all_to_all | solution.py:46
  46.3 6.4 %all-to-all-start.1 = ((bf16[128,24,128]{0,2,1:T(8,128)(2,1)}), bf16[128,24,128]{0,2,1:T(8,128)(2,1)S(1)}, u32[]{:S(2)}, u32[]{:S(2)}) async-start(bf16[128,24,128]{0,2,1:T(8,128)(2,1)} %bitcast.111), calls=%async_computation.1 | async-start | bytes 1572864 | tf_op jit(solution)/shard_map/all_to_all | solution.py:47
  52.7 2.3 copy.70
  55.0 11.3 %all-to-all-done.1 = bf16[128,24,128]{0,2,1:T(8,128)(2,1)S(1)} async-done(((bf16[128,24,128]{0,2,1:T(8,128)(2,1)}), bf16[128,24,128]{0,2,1:T(8,128)(2,1)S(1)}, u32[]{:S(2)}, u32[]{:S(2)}) %all-to-all-start.1) | async-done | bytes 786464 | tf_op jit(solution)/shard_map/all_to_all | solution.py:47
  66.3 7.3 %all-to-all-start.2 = ((bf16[128,24,128]{0,2,1:T(8,128)(2,1)}), bf16[128,24,128]{0,2,1:T(8,128)(2,1)}, u32[]{:S(2)}, u32[]{:S(2)}) async-start(bf16[128,24,128]{0,2,1:T(8,128)(2,1)} %bitcast.110), calls=%async_computation.2 | async-start | bytes 1572864 | tf_op jit(solution)/shard_map/all_to_all | solution.py:48
  73.7 1.6 broadcast_compare_fusion
  75.3 1.4 copy.62
  78.4 1.4 copy.64
  80.3 9.1 %all-to-all-done.2 = bf16[128,24,128]{0,2,1:T(8,128)(2,1)} async-done(((bf16[128,24,128]{0,2,1:T(8,128)(2,1)}), bf16[128,24,128]{0,2,1:T(8,128)(2,1)}, u32[]{:S(2)}, u32[]{:S(2)}) %all-to-all-start.2) | async-done | bytes 786464 | tf_op jit(solution)/shard_map/all_to_all | solution.py:48
  89.4 2.3 copy.72
  91.7 1.4 convert_element_type.96
  93.3 2.3 copy-done.3
  97.6 1.4 multiply_convert_fusion.1
  99.0 10.7 %fusion.54 = (f32[3,1024]{1,0:T(4,128)S(1)}, f32[3,1024,1024]{1,2,0:T(8,128)}) fusion(pred[1024,1024]{0,1:T(8,128)(4,1)S(1)} %copy-done.12, bf16[1024,3,128]{0,2,1:T(8,128)(2,1)S(1)} %get-tuple-element.32, bf16[1024,3,128]{0,2,1:T(8,128)(2,1)} %get-tuple-element.33), kind=kOutput, calls=%fused_computation.65 | convolution fusion | flops 817890304 | bytes 15216640 | tf_op jit(solution)/shard_map/sub | solution.py:33
  109.7 6.7 %all-gather.2.cloned.1.call-done = bf16[3072,768]{1,0:T(8,128)(2,1)} async-done(((bf16[96,768]{1,0:T(8,128)(2,1)}), bf16[3072,768]{1,0:T(8,128)(2,1)}) %all-gather.2.cloned.1.call-update) | async-done | bytes 4718608 | tf_op jit(solution)/shard_map/all_gather | solution.py:65
  116.4 9.3 %convolution_convert_fusion = bf16[1024,3072]{1,0:T(8,128)(2,1)} fusion(bf16[1024,768]{1,0:T(8,128)(2,1)S(1)} %copy-done, bf16[3072,768]{1,0:T(8,128)(2,1)} %all-gather.2.cloned.1.call-done), kind=kOutput, calls=%fused_computation.14 | convolution fusion | flops 4834983936 | bytes 12582912 | tf_op jit(solution)/shard_map/ld,cd->lc/dot_general | solution.py:62
  125.7 8.7 %copy.93 = bf16[1024,3072]{0,1:T(8,128)(2,1)} copy(bf16[1024,3072]{1,0:T(8,128)(2,1)} %convolution_convert_fusion) | data formatting | bytes 12582912
  135.5 5.7 %fusion.38 = bf16[3,1024,128]{1,2,0:T(8,128)(2,1)S(1)} fusion(bf16[1024,3,128]{2,0,1:T(8,128)(2,1)S(1)} %bitcast.108, f32[3,1024,1024]{1,2,0:T(8,128)} %get-tuple-element.29, f32[3,1024]{1,0:T(4,128)S(1)} %get-tuple-element.28), kind=kOutput, calls=%fused_computation.45 | convolution fusion | flops 811991040 | bytes 14168064 | tf_op jit(solution)/shard_map/tgi,itp->gtp/dot_general | solution.py:58
  142.0 218.8 %all_to_all.41 = bf16[8,1024,384]{1,2,0:T(8,128)(2,1)S(1)} all-to-all(bf16[8,1024,384]{1,2,0:T(8,128)(2,1)S(1)} %stack.3), channel_id=1, replica_groups=mesh['fsdp'=32,'seq'=8] {'seq'}, dimensions={0} | all-to-all | bytes 12582912 | tf_op jit(solution)/shard_map/all_to_all | solution.py:96
  360.8 7.4 %fusion.59 = f32[3072,768]{1,0:T(8,128)} fusion(bf16[1024,3072]{0,1:T(8,128)(2,1)S(1)} %bitcast.107, bf16[1024,768]{1,0:T(8,128)(2,1)S(1)} %copy-done), kind=kOutput, calls=%fused_computation.66 | convolution fusion | flops 4831838208 | bytes 17301504 | tf_op jit(solution)/shard_map/lc,ld->cd/dot_general | solution.py:93
  368.2 19.8 %reduce-scatter.7.cloned.1.call-done = bf16[384,1024]{1,0:T(8,128)(2,1)} async-done(((bf16[3072,1024]{1,0:T(8,128)(2,1)}), bf16[384,1024]{1,0:T(8,128)(2,1)}) %reduce-scatter.7.cloned.1.call-update) | async-done | bytes 786448
  388.0 7.5 %fusion.60 = f32[3,1024,1024]{1,2,0:T(8,128)} fusion(bf16[1024,3,128]{2,0,1:T(8,128)(2,1)S(1)} %bitcast.109, bf16[1024,3,128]{0,2,1:T(8,128)(2,1)} %bitcast.112), kind=kOutput, calls=%fused_computation.67 | convolution fusion | flops 805306368 | bytes 14155776 | tf_op jit(solution)/shard_map/krt,irt->rki/dot_general | solution.py:78
  395.5 19.6 %bitcast_reduce_fusion.1 = (f32[1024,3]{0,1:T(4,128)S(1)}, f32[1024,3]{0,1:T(4,128)S(1)}, f32[3,128,1024]{2,1,0:T(8,128)}) fusion(f32[1024,3]{0,1:T(4,128)S(1)} %rsqrt_bitcast_fusion.1, f32[1024,3]{0,1:T(4,128)S(1)} %get-tuple-element.25, f32[8,3,16,8,128]{4,3,2,1,0:T(8,128)S(1)} %bitcast.105, f32[128]{0:T(128)S(1)} %copy-done.16, ...), kind=kOutput, calls=%fused_computation.33 | convolution fusion | flops 829683712 | bytes 29159936 | tf_op jit(solution)/shard_map/tgi,itp->gtp/dot_general | solution.py:85
  415.2 1.8 fusion.27
  418.7 19.6 %bitcast_reduce_fusion = (f32[1024,3]{0,1:T(4,128)S(1)}, f32[1024,3]{0,1:T(4,128)S(1)}, f32[3,128,1024]{2,1,0:T(8,128)}) fusion(f32[1024,3]{0,1:T(4,128)S(1)} %rsqrt_bitcast_fusion, f32[1024,3]{0,1:T(4,128)S(1)} %get-tuple-element.26, f32[8,3,16,8,128]{4,3,2,1,0:T(8,128)S(1)} %bitcast.102, f32[128]{0:T(128)S(1)} %copy-done.17, ...), kind=kOutput, calls=%fused_computation.26 | convolution fusion | flops 829683712 | bytes 29159936 | tf_op jit(solution)/shard_map/jpw,pjy->wjy/dot_general | solution.py:88
  438.3 1.7 fusion.23
  441.2 7.1 %fusion.43 = bf16[1024,3,128]{0,2,1:T(8,128)(2,1)S(1)} fusion(bf16[1024,3,128]{0,2,1:T(8,128)(2,1)S(1)} %bitcast.113, f32[3,1024,1024]{1,2,0:T(8,128)} %get-tuple-element.29, f32[3,1024]{1,0:T(4,128)S(1)} %get-tuple-element.28), kind=kOutput, calls=%fused_computation.47 | convolution fusion | flops 811991040 | bytes 14168064 | tf_op jit(solution)/shard_map/jpw,pjy->wjy/dot_general | solution.py:72
  448.3 1.2 copy.81
  449.4 96.8 %reduce-scatter.5.cloned.1.call-done = f32[96,768]{1,0:T(8,128)} async-done(((f32[3072,768]{1,0:T(8,128)}), f32[96,768]{1,0:T(8,128)}) %reduce-scatter.5.cloned.1.call-update) | async-done | bytes 294928 | tf_op jit(solution)/shard_map/reduce_scatter | solution.py:101
  546.2 1.7 broadcast_multiply_fusion
  (58 shorter events, 10.9 us)
Async XLA Ops:
  7.2 109.2 %copy-start = (bf16[1024,768]{1,0:T(8,128)(2,1)S(1)}, bf16[1024,768]{1,0:T(8,128)(2,1)}, u32[]{:S(2)}) copy-start(bf16[1024,768]{1,0:T(8,128)(2,1)} %param.15) | copy-start | bytes 4718596
  7.2 109.2 %all-gather.2.cloned.1.call-start = ((), (), s32[]{:S(2)}) async-start(), calls=%async_computation.6 | async-start | bytes 4866048 | tf_op jit(solution)/shard_map/all_gather | solution.py:65
  7.9 13.9 %copy-start.14 = (bf16[128,3072]{1,0:T(8,128)(2,1)S(1)}, bf16[128,3072]{1,0:T(8,128)(2,1)}, u32[]{:S(2)}) copy-start(bf16[128,3072]{1,0:T(8,128)(2,1)} %param.9) | copy-start | bytes 2359300
  10.3 36.0 %all-to-all-start = ((bf16[128,24,128]{0,2,1:T(8,128)(2,1)}), bf16[128,24,128]{0,2,1:T(8,128)(2,1)S(1)}, u32[]{:S(2)}, u32[]{:S(2)}) async-start(bf16[128,24,128]{0,2,1:T(8,128)(2,1)} %bitcast), calls=%async_computation | async-start | bytes 1572864 | tf_op jit(solution)/shard_map/all_to_all | solution.py:46
  46.3 8.7 %copy-start.8 = (bf16[128,24,128]{0,2,1:T(8,128)(2,1)}, bf16[128,24,128]{0,2,1:T(8,128)(2,1)S(1)}, u32[]{:S(2)}) copy-start(bf16[128,24,128]{0,2,1:T(8,128)(2,1)S(1)} %all-to-all-done) | copy-start | bytes 2359300
  46.3 20.0 %all-to-all-start.1 = ((bf16[128,24,128]{0,2,1:T(8,128)(2,1)}), bf16[128,24,128]{0,2,1:T(8,128)(2,1)S(1)}, u32[]{:S(2)}, u32[]{:S(2)}) async-start(bf16[128,24,128]{0,2,1:T(8,128)(2,1)} %bitcast.111), calls=%async_computation.1 | async-start | bytes 1572864 | tf_op jit(solution)/shard_map/all_to_all | solution.py:47
  52.7 21.0 %copy-start.15 = (s32[1,1024]{1,0:T(1,128)S(1)}, s32[1,1024]{1,0:T(1,128)}, u32[]{:S(2)}) copy-start(s32[1,1024]{1,0:T(1,128)} %param.11) | copy-start | bytes 12292
  66.3 7.3 %copy-start.9 = (bf16[128,24,128]{0,2,1:T(8,128)(2,1)}, bf16[128,24,128]{0,2,1:T(8,128)(2,1)S(1)}, u32[]{:S(2)}) copy-start(bf16[128,24,128]{0,2,1:T(8,128)(2,1)S(1)} %all-to-all-done.1) | copy-start | bytes 2359300
  66.3 23.1 %all-to-all-start.2 = ((bf16[128,24,128]{0,2,1:T(8,128)(2,1)}), bf16[128,24,128]{0,2,1:T(8,128)(2,1)}, u32[]{:S(2)}, u32[]{:S(2)}) async-start(bf16[128,24,128]{0,2,1:T(8,128)(2,1)} %bitcast.110), calls=%async_computation.2 | async-start | bytes 1572864 | tf_op jit(solution)/shard_map/all_to_all | solution.py:48
  73.7 314.4 %reduce-scatter.7.cloned.1.call-start = ((), (), s32[]{:S(2)}) async-start(), calls=%async_computation.8 | async-start | bytes 7077888
  76.7 1.2 copy-start.2
  91.7 1.4 copy-start.10
  93.1 4.5 copy-start.6
  93.1 2.5 copy-start.3
  93.3 4.3 copy-start.4
  95.6 1.9 copy-start.16
  95.6 1.9 copy-start.17
  97.6 1.4 copy-start.12
  134.4 1.1 copy-start.11
  134.4 411.8 %reduce-scatter.5.cloned.1.call-start = ((), (), s32[]{:S(2)}) async-start(), calls=%async_computation.7 | async-start | bytes 9732096 | tf_op jit(solution)/shard_map/reduce_scatter | solution.py:101
  388.0 7.5 %copy-start.7 = (f32[128,24,128]{0,2,1:T(8,128)S(1)}, f32[128,24,128]{0,2,1:T(8,128)}, u32[]{:S(2)}) copy-start(f32[128,24,128]{0,2,1:T(8,128)} %copy-done.6) | copy-start | bytes 4718596
  417.0 1.7 copy-start.5
  440.1 1.2 copy-start.13
  441.2 106.7 %copy-start.1 = (bf16[1024,768]{1,0:T(8,128)(2,1)S(1)}, bf16[1024,768]{1,0:T(8,128)(2,1)}, u32[]{:S(2)}) copy-start(bf16[1024,768]{1,0:T(8,128)(2,1)} %param.15) | copy-start | bytes 4718596
Sparse Core Ops, SparseCore 0:
  9.9 106.4 all-gather.1
  134.5 253.4 reduce-scatter.6
  390.8 155.4 reduce-scatter.4
